TPU v7x, 512 devices: a whole 4x8x8 slice. The times are simulated.
512 devices in a mesh: row: 16 (over x_lo, z), col: 32 (over y, x_hi, core).
Axes of the slice: x: 4 (x_hi: 2, x_lo: 2; x = x_hi * 2 + x_lo), y: 8, z: 8, core: 2. Of those that a mesh axis runs over, the one named last changes fastest.
Arguments:
- protocols: float32 [20, 65536], P(None, ('row', 'col')), may hold values from -6 to 6
- w_in: float32 [20, 256], replicated, may hold values from -1.25 to 1.25
- b_in: float32 [256], replicated, may hold values from -3 to 3
- w_out: float32 [256, 64], replicated, may hold values from -0.21875 to 0.21875
- solved: float32 [32, 65536], P(None, ('row', 'col')), may hold values from -0.5 to 0.5
- probes: float32 [32, 65536], P(None, ('row', 'col')), may hold values from -6 to 6
- window_blocks: int32 [16], replicated, may hold values from 0 to 31
Outputs:
- col_grad: float32 [64, 65536], P(None, ('row', 'col'))
- grad_in: float32 [20, 256], replicated
- grad_bias: float32 [256], replicated
- grad_out: float32 [256, 64], replicated
Inputs may be any that keep to these rules, and one draw needn't show every extreme that they name: Window block r is the 128 protocols held at index r of row and index window_blocks[r] of col.
All inputs are finite; a program needn't handle non-finite values.
Results may differ from a plain program's by a relative error of at most 0.0003.
Values sent between devices are 32-bit elements; how exact they have to be, the bound alone decides.
A program may use at most 64 MiB of HBM per device.

v0:
```python
import jax
import jax.numpy as jnp
from jax import lax
from jax.sharding import PartitionSpec as P

HIGHEST = lax.Precision.HIGHEST


def spread(value, axis, source):
    kept = jnp.where(lax.axis_index(axis) == source, value, 0).astype(value.dtype)
    return lax.psum(kept, axis)


def tile_pass(first_feat, first_vec, second_feat, second_vec):
    first_norm = jnp.sum(first_feat * first_feat, 0)
    second_norm = jnp.sum(second_feat * second_feat, 0)
    cross = jnp.einsum("fi,fj->ij", first_feat, second_feat, precision=HIGHEST)
    kern = jnp.exp(-0.5 * (first_norm[:, None] + second_norm[None, :] - 2.0 * cross))
    weigh = jnp.einsum("qi,qj->ij", first_vec, second_vec, precision=HIGHEST) * kern
    first_grad = (
        jnp.einsum("fj,ij->fi", second_feat, weigh, precision=HIGHEST)
        - first_feat * jnp.sum(weigh, 1)[None, :]
    )
    second_grad = (
        jnp.einsum("fi,ij->fj", first_feat, weigh, precision=HIGHEST)
        - second_feat * jnp.sum(weigh, 0)[None, :]
    )
    return (first_grad, second_grad)


def blocked(first_feat, first_vec, second_feat, second_vec):
    width = second_feat.shape[1]
    block_width = 1024
    count = width // block_width
    split_feat = second_feat.reshape(second_feat.shape[0], count, block_width).transpose(1, 0, 2)
    split_vec = second_vec.reshape(second_vec.shape[0], count, block_width).transpose(1, 0, 2)

    def partial_pass(running, pair):
        first_part, second_part = tile_pass(first_feat, first_vec, pair[0], pair[1])
        return (running + first_part, second_part)

    first_grad, second_parts = lax.scan(
        partial_pass, jnp.zeros_like(first_feat), (split_feat, split_vec)
    )
    return (first_grad, second_parts.transpose(1, 0, 2).reshape(second_feat.shape[0], width))


def hidden_of(w_in, b_in, inputs):
    return jnp.tanh(jnp.einsum("ph,pn->hn", w_in, inputs, precision=HIGHEST) + b_in[:, None])


def backprop(w_out, inputs, hidden, grads):
    grad_out = jnp.einsum("hn,fn->hf", hidden, grads, precision=HIGHEST)
    grad_hidden = jnp.einsum("hf,fn->hn", w_out, grads, precision=HIGHEST)
    grad_pre = grad_hidden * (1.0 - hidden * hidden)
    grad_in = jnp.einsum("pn,hn->ph", inputs, grad_pre, precision=HIGHEST)
    return (grad_in, jnp.sum(grad_pre, 1), grad_out)


def window_total(partial_grad):
    return lax.psum(partial_grad, "col")


def per_device(protocols, w_in, b_in, w_out, solved, probes, window_blocks):
    hidden = hidden_of(w_in, b_in, protocols)
    features = jnp.einsum("hf,hn->fn", w_out, hidden, precision=HIGHEST)
    owner_col = window_blocks[lax.axis_index("row")]
    is_owner = lax.axis_index("col") == owner_col
    window = (spread(features, "col", owner_col), spread(solved, "col", owner_col))
    win_part, col_part = blocked(
        window[0],
        window[1],
        lax.all_gather(features, "row", axis=1, tiled=True),
        lax.all_gather(probes, "row", axis=1, tiled=True),
    )
    col_grad = lax.psum_scatter(col_part, "row", scatter_dimension=1, tiled=True)
    summed = window_total(win_part)
    own_total = col_grad + jnp.where(is_owner, summed, jnp.zeros_like(summed))
    terms = backprop(w_out, protocols, hidden, own_total)
    grad_in, grad_bias, grad_out = lax.psum((terms[0], terms[1], terms[2]), ("row", "col"))
    return (col_grad, grad_in, grad_bias, grad_out)


def solution(mesh):
    in_specs = (
        P(None, ("row", "col")),
        P(),
        P(),
        P(),
        P(None, ("row", "col")),
        P(None, ("row", "col")),
        P(),
    )
    out_specs = (P(None, ("row", "col")), P(), P(), P())
    return jax.shard_map(
        per_device, mesh=mesh, in_specs=in_specs, out_specs=out_specs, check_vma=False
    )
```

profile of v0, /device:TPU:1, one launch (start us, length us, event | category | flops | bytes accessed | tf_op | source)
XLA Modules:
  0.0 622.4 jit_solution(2819054057416116378)
XLA Ops:
  7.2 0.0 copy-start
  7.2 0.0 copy-start.5
  7.2 0.0 reduce-scatter.2.cloned.1.call-start
  7.3 0.0 copy-start.7
  7.3 0.0 copy-start.3
  7.3 0.6 copy-done.7
  7.9 0.6 dynamic_slice.15
  9.2 0.0 copy-done.5
  9.2 0.0 copy-start.2
  9.2 0.0 copy-start.6
  9.2 0.0 copy-done.3
  9.2 0.7 copy-done.2
  9.9 0.0 copy-done.6
  9.9 0.3 fusion.17
  10.2 0.0 copy-done
  10.2 0.3 broadcast_select_fusion
  10.5 129.4 %all-reduce.1 = (f32[32,128]{1,0:T(8,128)S(1)}, f32[64,128]{1,0:T(8,128)S(1)}) all-reduce(f32[32,128]{1,0:T(8,128)S(1)} %broadcast_select_fusion.1, f32[64,128]{1,0:T(8,128)S(1)} %get-tuple-element.153), channel_id=1, replica_groups=mesh['row'=16,'col'=32] {'col'}, use_global_device_ids=true, to_apply=%region_1.2 | all-reduce | flops 12288 | bytes 98304 | tf_op jit(solution)/shard_map/psum | solution.py:11
  139.9 0.0 copy-start.4
  139.9 0.7 copy-done.4
  140.6 32.7 %all_gather.7 = f32[32,2048]{1,0:T(8,128)S(1)} all-gather(f32[32,128]{1,0:T(8,128)S(1)} %copy-done.4), channel_id=1, replica_groups=mesh['row'=16,'col'=32] {'row'}, dimensions={1}, use_global_device_ids=true | all-gather | bytes 278528 | tf_op jit(solution)/shard_map/all_gather | solution.py:74
  173.3 0.2 reshape.23
  173.5 26.2 %all_gather.6 = f32[64,2048]{1,0:T(8,128)S(1)} all-gather(f32[64,128]{1,0:T(8,128)S(1)} %get-tuple-element.154), channel_id=1, replica_groups=mesh['row'=16,'col'=32] {'row'}, dimensions={1}, use_global_device_ids=true | all-gather | bytes 557056 | tf_op jit(solution)/shard_map/all_gather | solution.py:73
  199.7 7.0 %while.15 = (s32[]{:T(128)}, f32[64,128]{1,0:T(8,128)S(1)}, f32[2,64,1024]{2,1,0:T(8,128)S(1)}, f32[2,64,1024]{2,1,0:T(8,128)S(1)}, f32[2,32,1024]{2,0,1:T(2,128...) while((s32[]{:T(128)}, f32[64,128]{1,0:T(8,128)S(1)}, ...), condition=%wide.region_7.8_spmd.clone, body=%wide.region_3.0_spmd.clone.sunk | while | flops 353531776 | bytes 4523659 | solution.py:42
  199.8 0.1 constant_dynamic-slice_fusion.2
  199.9 1.0 fusion.56
  201.0 1.1 fusion.57
  202.1 0.5 fusion.58
  202.5 0.7 fusion.59
  203.3 0.1 constant_dynamic-slice_fusion.2
  203.4 1.0 fusion.56
  204.5 1.1 fusion.57
  205.6 0.5 fusion.58
  206.0 0.7 fusion.59
  206.7 0.8 copy.18
  207.6 0.0 reduce-scatter.2.cloned.1.call-update
  207.6 0.0 all-reduce.4.cloned.1.call-start
  207.7 142.1 %psum.44 = f32[64,128]{1,0:T(8,128)S(1)} all-reduce(f32[64,128]{1,0:T(8,128)S(1)} %get-tuple-element.94), channel_id=1, replica_groups=mesh['row'=16,'col'=32] {'col'}, use_global_device_ids=true, to_apply=%region_9.10 | all-reduce | flops 8192 | bytes 65536 | tf_op jit(solution)/shard_map/psum | solution.py:61
  349.8 0.0 reduce-scatter.2.cloned.1.call-done
  349.8 1.6 fusion.18
  351.4 0.0 copy-start.1
  351.4 0.0 all-reduce.4.cloned.1.call-update
  351.4 0.7 copy-done.1
  352.2 0.3 fusion.22
  352.5 0.2 convolution_bitcast_fusion.4
  352.7 101.5 %all-reduce = (f32[20,256]{1,0:T(8,128)}, f32[256]{0:T(256)}) all-reduce(f32[20,256]{1,0:T(8,128)S(1)} %convolution_bitcast_fusion.4, f32[256]{0:T(256)S(1)} %get-tuple-element.155), channel_id=1, replica_groups=mesh['row'=16,'col'=32] {'row','col'}, use_global_device_ids=true, to_apply=%region_10.11 | all-reduce | flops 5376 | bytes 43008 | tf_op jit(solution)/shard_map/psum | solution.py:80
  454.2 159.8 %all-reduce.4.cloned.1.call-done = f32[256,64]{0,1:T(8,128)} async-done(((f32[256,64]{0,1:T(8,128)}), f32[256,64]{0,1:T(8,128)}) %all-reduce.4.cloned.1.call-update) | async-done | bytes 65552 | tf_op jit(solution)/shard_map/psum | solution.py:80
  614.1 1.5 copy.38
  (7 shorter events, 0.1 us)
Async XLA Ops:
  7.2 3.0 copy-start
  7.2 2.0 copy-start.5
  7.2 342.6 %reduce-scatter.2.cloned.1.call-start = ((), (), s32[]{:S(2)}) async-start(), calls=%async_computation.1 | async-start | bytes 557056 | tf_op jit(solution)/shard_map/reduce_scatter | solution.py:76
  7.3 0.7 copy-start.7
  7.3 1.9 copy-start.3
  9.2 0.7 copy-start.2
  9.2 0.7 copy-start.6
  139.9 0.7 copy-start.4
  207.6 406.5 %all-reduce.4.cloned.1.call-start = ((), (), s32[]{:S(2)}) async-start(), calls=%async_computation.2 | async-start | bytes 131072 | tf_op jit(solution)/shard_map/psum | solution.py:80
  351.4 0.8 copy-start.1
Sparse Core Ops, SparseCore 0:
  207.7 75.7 reduce-scatter.1
  351.6 262.4 all-reduce.3
where the time goes:
time: 623 us; the launch traced here: 622 us
  blocking collectives  432 us (69%)
  waiting for transfers between devices  160 us (26%)
  between operations  14.8 us (2%)
  matrix products  9.29 us (1%)
    psum x1, waiting for transfers between devices, per_device(): lax.psum((terms[0], terms[1], terms[2]), ('row', 'col'))  160 us
    psum x1, blocking collectives, window_total(): return lax.psum(partial_grad, 'col')  142 us
    psum x1, blocking collectives, spread(): return lax.psum(kept, axis)  129 us
    psum x1, blocking collectives, per_device(): lax.psum((terms[0], terms[1], terms[2]), ('row', 'col'))  102 us
    all_gather x1, blocking collectives, per_device(): lax.all_gather(probes, 'row', axis=1, tiled=True)  32.7 us
    all_gather x1, blocking collectives, per_device(): lax.all_gather(features, 'row', axis=1, tiled=True)  26.2 us
  transfers between devices with their start and end apart: 2, of which 1 were waited for; matrix products, arithmetic and copies ran while one was open for 0% of the time, Pallas kernels for 0%

commit v1 on v0

--- a/solution.py
+++ b/solution.py
@@ -71,7 +71,9 @@
         window[0],
         window[1],
         lax.all_gather(features, "row", axis=1, tiled=True),
-        lax.all_gather(probes, "row", axis=1, tiled=True),
+        jnp.concatenate(
+            lax.all_to_all(jnp.stack([probes] * lax.axis_size("row")), "row", 0, 0), axis=1
+        ),
     )
     col_grad = lax.psum_scatter(col_part, "row", scatter_dimension=1, tiled=True)
     summed = window_total(win_part)

time: 623 us -> 595 us (0.955)
  blocking collectives: 432 us -> 388 us
  starting transfers between devices: 0.08 us -> 12.1 us
    all_gather x1 -> x0, blocking collectives: 32.7 us -> none  [per_device(): lax.all_gather(probes, 'row', axis=1, tiled=True)]
    psum x1, blocking collectives: 142 us -> 129 us  [window_total(): return lax.psum(partial_grad, 'col')]
    all_to_all x0 -> x1, starting transfers between devices: none -> 12 us  [per_device(): lax.all_to_all(jnp.stack([probes] * lax.axis_size('row')), 'row', 0, 0)]
  transfers between devices with their start and end apart: 2 -> 3, of which waited for: 1 -> 1; matrix products, arithmetic and copies ran while one was open for 0% -> 0% of each run, Pallas kernels for 0% -> 0%
where the time goes in v1:
time: 595 us; the launch traced here: 594 us
  blocking collectives  388 us (65%)
  waiting for transfers between devices  162 us (27%)
  between operations  14.8 us (2%)
  starting transfers between devices  12.1 us (2%)
  matrix products  9.29 us (2%)
  local copies, waits for them, and re-layouts  6.99 us (1%)
    psum x1, waiting for transfers between devices, per_device(): lax.psum((terms[0], terms[1], terms[2]), ('row', 'col'))  162 us
    psum x1, blocking collectives, spread(): return lax.psum(kept, axis)  131 us
    psum x1, blocking collectives, window_total(): return lax.psum(partial_grad, 'col')  129 us
    psum x1, blocking collectives, per_device(): lax.psum((terms[0], terms[1], terms[2]), ('row', 'col'))  99.2 us
    all_gather x1, blocking collectives, per_device(): lax.all_gather(features, 'row', axis=1, tiled=True)  29.5 us
    all_to_all x1, starting transfers between devices, per_device(): lax.all_to_all(jnp.stack([probes] * lax.axis_size('row')), 'row', 0, 0)  12 us
  transfers between devices with their start and end apart: 3, of which 1 were waited for; matrix products, arithmetic and copies ran while one was open for 0% of the time, Pallas kernels for 0%

profile of v1, /device:TPU:1, one launch (start us, length us, event | category | flops | bytes accessed | tf_op | source)
XLA Modules:
  0.0 593.9 jit_solution(7067267734903227665)
XLA Ops:
  7.2 0.0 copy-start
  7.2 1.5 stack.2
  8.6 0.0 copy-start.3
  8.6 12.0 %all-to-all-start = ((f32[16,32,128]{2,1,0:T(8,128)}), f32[16,32,128]{2,1,0:T(8,128)S(1)}, u32[]{:S(2)}, u32[]{:S(2)}) async-start(f32[16,32,128]{2,1,0:T(8,128)} %stack.2), calls=%async_computation | async-start | bytes 524288 | tf_op jit(solution)/shard_map/all_to_all | solution.py:75
  20.7 0.0 reduce-scatter.2.cloned.1.call-start
  20.7 0.0 copy-start.2
  20.8 0.0 copy-start.6
  20.8 0.6 copy-done.6
  21.4 0.6 dynamic_slice.15
  22.0 0.0 copy-start.5
  22.7 0.0 copy-done.3
  22.7 0.0 copy-done.2
  22.7 0.0 copy-done.5
  22.7 0.3 fusion.17
  23.0 0.0 copy-done
  23.0 0.3 broadcast_select_fusion
  23.3 29.5 %all_gather.3 = f32[64,2048]{1,0:T(8,128)S(1)} all-gather(f32[64,128]{1,0:T(8,128)S(1)} %get-tuple-element.162), channel_id=1, replica_groups=mesh['row'=16,'col'=32] {'row'}, dimensions={1}, use_global_device_ids=true | all-gather | bytes 557056 | tf_op jit(solution)/shard_map/all_gather | solution.py:73
  52.8 0.0 copy-start.4
  52.8 0.7 copy-done.4
  53.5 131.2 %all-reduce.1 = (f32[32,128]{1,0:T(8,128)S(1)}, f32[64,128]{1,0:T(8,128)S(1)}) all-reduce(f32[32,128]{1,0:T(8,128)S(1)} %broadcast_select_fusion.1, f32[64,128]{1,0:T(8,128)S(1)} %get-tuple-element.161), channel_id=1, replica_groups=mesh['row'=16,'col'=32] {'col'}, use_global_device_ids=true, to_apply=%region_1.2 | all-reduce | flops 12288 | bytes 98304 | tf_op jit(solution)/shard_map/psum | solution.py:11
  184.7 0.0 all-to-all-done
  184.7 0.2 copy.17
  184.9 0.1 reshape_reshape.3
  185.1 7.0 %while.15 = (s32[]{:T(128)}, f32[64,128]{1,0:T(8,128)S(1)}, f32[2,64,1024]{2,1,0:T(8,128)S(1)}, f32[2,64,1024]{2,1,0:T(8,128)S(1)}, f32[2,32,1024]{2,0,1:T(2,128...) while((s32[]{:T(128)}, f32[64,128]{1,0:T(8,128)S(1)}, ...), condition=%wide.region_7.8_spmd.clone, body=%wide.region_3.0_spmd.clone.sunk | while | flops 353531776 | bytes 4523659 | solution.py:42
  185.1 0.1 constant_dynamic-slice_fusion.2
  185.2 1.0 fusion.56
  186.3 1.1 fusion.57
  187.4 0.5 fusion.58
  187.8 0.7 fusion.59
  188.6 0.1 constant_dynamic-slice_fusion.2
  188.7 1.0 fusion.56
  189.8 1.1 fusion.57
  190.9 0.5 fusion.58
  191.3 0.7 fusion.59
  192.1 0.8 copy.22
  192.9 0.0 reduce-scatter.2.cloned.1.call-update
  192.9 0.0 all-reduce.4.cloned.1.call-start
  193.0 128.5 %psum.44 = f32[64,128]{1,0:T(8,128)S(1)} all-reduce(f32[64,128]{1,0:T(8,128)S(1)} %get-tuple-element.94), channel_id=1, replica_groups=mesh['row'=16,'col'=32] {'col'}, use_global_device_ids=true, to_apply=%region_9.10 | all-reduce | flops 8192 | bytes 65536 | tf_op jit(solution)/shard_map/psum | solution.py:61
  321.5 0.0 reduce-scatter.2.cloned.1.call-done
  321.5 1.6 fusion.18
  323.1 0.0 copy-start.1
  323.1 0.0 all-reduce.4.cloned.1.call-update
  323.1 0.7 copy-done.1
  323.9 0.3 fusion.22
  324.2 0.2 convolution_bitcast_fusion.4
  324.4 99.2 %all-reduce = (f32[20,256]{1,0:T(8,128)}, f32[256]{0:T(256)}) all-reduce(f32[20,256]{1,0:T(8,128)S(1)} %convolution_bitcast_fusion.4, f32[256]{0:T(256)S(1)} %get-tuple-element.163), channel_id=1, replica_groups=mesh['row'=16,'col'=32] {'row','col'}, use_global_device_ids=true, to_apply=%region_10.11 | all-reduce | flops 5376 | bytes 43008 | tf_op jit(solution)/shard_map/psum | solution.py:82
  423.6 162.0 %all-reduce.4.cloned.1.call-done = f32[256,64]{0,1:T(8,128)} async-done(((f32[256,64]{0,1:T(8,128)}), f32[256,64]{0,1:T(8,128)}) %all-reduce.4.cloned.1.call-update) | async-done | bytes 65552 | tf_op jit(solution)/shard_map/psum | solution.py:82
  585.6 1.5 copy.42
  (7 shorter events, 0.1 us)
Async XLA Ops:
  7.2 15.9 %copy-start = (f32[256,64]{0,1:T(8,128)S(1)}, f32[256,64]{0,1:T(8,128)}, u32[]{:S(2)}) copy-start(f32[256,64]{0,1:T(8,128)} %param.12) | copy-start | bytes 196612
  8.6 14.0 %copy-start.3 = (f32[20,256]{1,0:T(8,128)S(1)}, f32[20,256]{1,0:T(8,128)}, u32[]{:S(2)}) copy-start(f32[20,256]{1,0:T(8,128)} %param.10) | copy-start | bytes 61444
  8.6 176.1 %all-to-all-start = ((f32[16,32,128]{2,1,0:T(8,128)}), f32[16,32,128]{2,1,0:T(8,128)S(1)}, u32[]{:S(2)}, u32[]{:S(2)}) async-start(f32[16,32,128]{2,1,0:T(8,128)} %stack.2), calls=%async_computation | async-start | bytes 524288 | tf_op jit(solution)/shard_map/all_to_all | solution.py:75
  20.7 300.8 %reduce-scatter.2.cloned.1.call-start = ((), (), s32[]{:S(2)}) async-start(), calls=%async_computation.2 | async-start | bytes 557056 | tf_op jit(solution)/shard_map/reduce_scatter | solution.py:78
  20.7 1.9 copy-start.2
  20.8 0.7 copy-start.6
  22.0 0.7 copy-start.5
  52.8 0.7 copy-start.4
  192.9 392.7 %all-reduce.4.cloned.1.call-start = ((), (), s32[]{:S(2)}) async-start(), calls=%async_computation.3 | async-start | bytes 131072 | tf_op jit(solution)/shard_map/psum | solution.py:82
  323.1 0.8 copy-start.1
Sparse Core Ops, SparseCore 0:
  193.0 62.3 reduce-scatter.1
  323.2 262.2 all-reduce.3
